TPU v7x, 128 devices: a whole 4x4x4 slice. The times are simulated.
128 devices in a mesh: blk: 32 (over x, y, core), mp: 4 (over z).
Axes of the slice: x: 4, y: 4, z: 4, core: 2. Of those that a mesh axis runs over, the one named last changes fastest.
Arguments:
- hidden: bfloat16 [144, 3584], replicated, may hold values from -6 to 6
- medusa_w: bfloat16 [2, 3584, 3584], P(None, 'blk', 'mp'), may hold values from -0.09375 to 0.09375
- embedding: bfloat16 [131072, 3584], P(('blk', 'mp')), may hold values from -0.5 to 0.5
- cand_ids: int32 [2, 144, 10], replicated, may hold values from 0 to 131071
- tree_q: bfloat16 [12, 48, 4096], P(None, None, 'mp'), may hold values from -6 to 6
- tree_key_value: bfloat16 [2, 12, 48, 2048], P(None, None, None, 'mp'), may hold values from -6 to 6
- prompt_key_value: bfloat16 [2, 32, 2048, 2048], P(None, 'blk', None, 'mp'), may hold values from -6 to 6
- block_group: int32 [32], P('blk'), may hold values from 0 to 11, as said below
- block_len: int32 [32], P('blk'), may hold values from 1 to 2048
- block_empty: int32 [32], P('blk'), may hold values 0 or 1
- parents: int32 [12, 48], replicated, may hold values from 0 to 46, as said below
- out_weight: bfloat16 [4096, 3584], P('mp'), may hold values from -0.09375 to 0.09375
- post_gain: float32 [3584], replicated, may hold values from 0.5 to 1.5
- resid: bfloat16 [576, 3584], P('blk'), may hold values from -6 to 6
Outputs:
- draft_logprob: float32 [2, 144, 10], replicated
- layer_out: bfloat16 [576, 3584], P('blk')
Inputs may be any that keep to these rules, and one draw needn't show every extreme that they name: `block_group`: every group number from 0 to min(12, 32) - 1 owns at least one block. `parents`: entry 0 of each row is 0; entry i for i >= 1 is below i; some group's last token has parent 48 - 2.
All inputs are finite; a program needn't handle non-finite values. No bound on the sum of `block_empty` on one device may be relied on, other than what follows from the above.
Results may differ from a plain program's by a relative error of at most 0.005.
Values may be sent and summed in bfloat16 or wider, within the bound.
A program may use at most 128 MiB of HBM per device.

v0:
```python
import jax
import jax.numpy as jnp
from jax import lax
from jax.sharding import PartitionSpec as P

HEAD_SIZE = 256


def capped(values, limit):
    return limit * jnp.tanh(values / limit)


def ancestry(parents):
    count = parents.shape[1]
    column = jnp.arange(count, dtype=jnp.int32)
    linked = (parents[:, :, None] == column[None, None, :]) & (column[None, :, None] > 0)
    reach = jnp.eye(count, dtype=jnp.float32)[None] + linked.astype(jnp.float32)
    for sweep in range(count.bit_length()):
        reach = jnp.minimum(
            jnp.einsum("gij,gjk->gik", reach, reach, precision=lax.Precision.HIGHEST), 1.0
        )
    return reach


def attend(queries, keys, values, mask):
    rows = queries.shape[0]
    length = keys.shape[0]
    kv_heads = keys.shape[1] // HEAD_SIZE
    repeats = queries.shape[1] // keys.shape[1]
    query_view = queries.reshape(rows, kv_heads, repeats, HEAD_SIZE)
    key_view = keys.reshape(length, kv_heads, HEAD_SIZE)
    value_view = values.reshape(length, kv_heads, HEAD_SIZE)
    scores = jnp.einsum(
        "qhrd,khd->hrqk", query_view, key_view, preferred_element_type=jnp.float32
    ) * HEAD_SIZE ** (-0.5)
    weights = jnp.exp(capped(scores, 50.0)) * mask[None, None]
    denominator = jnp.sum(weights, -1).transpose(2, 0, 1).reshape(rows, kv_heads * repeats)
    numerator = jnp.einsum(
        "hrqk,khd->qhrd",
        weights.astype(jnp.bfloat16),
        value_view,
        preferred_element_type=jnp.float32,
    )
    return (numerator.reshape(rows, kv_heads * repeats * HEAD_SIZE), denominator)


def per_device(
    hidden,
    medusa_w,
    embedding,
    cand_ids,
    tree_q,
    tree_key_value,
    prompt_key_value,
    block_group,
    block_len,
    block_empty,
    parents,
    out_weight,
    post_gain,
    resid,
):
    units = medusa_w.shape[2]
    inner = jnp.einsum(
        "rd,mdu->mru",
        hidden,
        lax.all_gather(medusa_w, "blk", axis=1, tiled=True),
        preferred_element_type=jnp.float32,
    )
    own_cols = lax.dynamic_slice_in_dim(hidden, lax.axis_index("mp") * units, units, 1).astype(
        jnp.float32
    )
    fresh = (own_cols[None] + jax.nn.silu(inner)).astype(jnp.bfloat16)
    full_fresh = lax.all_gather(fresh, "mp", axis=2, tiled=True)
    logits = capped(
        jnp.einsum("mrd,vd->mrv", full_fresh, embedding, preferred_element_type=jnp.float32), 30.0
    )
    totals = jnp.sum(jnp.exp(logits), -1)
    vocab_dev = embedding.shape[0]
    first_id = lax.axis_index(("blk", "mp")) * vocab_dev
    local_ids = cand_ids - first_id
    match = local_ids[..., None] == jnp.arange(vocab_dev, dtype=jnp.int32)
    picked = jnp.sum(jnp.where(match, logits[:, :, None, :], 0.0), -1)
    totals, picked = lax.psum((totals, picked), ("blk", "mp"))
    draft_logprob = picked - jnp.log(totals)[..., None]
    groups, tree_size, features = tree_q.shape
    keys = prompt_key_value[0, 0]
    values = prompt_key_value[1, 0]
    length = keys.shape[0]
    group = block_group[0]
    key_ok = ((jnp.arange(length, dtype=jnp.int32) < block_len[0]) & (block_empty[0] == 0)).astype(
        jnp.float32
    )
    row_group = jnp.arange(groups * tree_size, dtype=jnp.int32) // tree_size
    mask = (row_group == group).astype(jnp.float32)[:, None] * key_ok[None, :]
    numer, denom = attend(tree_q.reshape(groups * tree_size, features), keys, values, mask)
    rows_dev = groups * tree_size // lax.axis_size("blk")
    first_row = lax.axis_index("blk") * rows_dev
    summed = lax.psum((numer, denom), "blk")
    numer = lax.dynamic_slice_in_dim(summed[0], first_row, rows_dev, 0)
    denom = lax.dynamic_slice_in_dim(summed[1], first_row, rows_dev, 0)
    reach = ancestry(parents)
    tree_numer, tree_denom = jax.vmap(attend)(tree_q, tree_key_value[0], tree_key_value[1], reach)
    heads_dev = tree_denom.shape[2]
    tree_numer = lax.dynamic_slice_in_dim(
        tree_numer.reshape(groups * tree_size, features), first_row, rows_dev, 0
    )
    tree_denom = lax.dynamic_slice_in_dim(
        tree_denom.reshape(groups * tree_size, heads_dev), first_row, rows_dev, 0
    )
    numer = numer + tree_numer
    denom = denom + tree_denom
    heads_out = (
        (numer.reshape(rows_dev, heads_dev, HEAD_SIZE) / denom[..., None])
        .reshape(rows_dev, features)
        .astype(jnp.bfloat16)
    )
    attn = lax.psum(jnp.dot(heads_out, out_weight, preferred_element_type=jnp.float32), "mp")
    normed = attn * lax.rsqrt(jnp.mean(attn * attn, -1, keepdims=True) + 1e-06) * post_gain
    layer_out = (normed + resid.astype(jnp.float32)).astype(jnp.bfloat16)
    return (draft_logprob, layer_out)


def solution(mesh):
    placed = (
        P(),
        P(None, "blk", "mp"),
        P(("blk", "mp"), None),
        P(),
        P(None, None, "mp"),
        P(None, None, None, "mp"),
        P(None, "blk", None, "mp"),
        P("blk"),
        P("blk"),
        P("blk"),
        P(),
        P("mp", None),
        P(),
        P("blk", None),
    )
    return jax.shard_map(
        per_device, mesh=mesh, in_specs=placed, out_specs=(P(), P("blk", None)), check_vma=False
    )
```

profile of v0, /device:TPU:1, one launch (start us, length us, event | category | flops | bytes accessed | tf_op | source)
XLA Modules:
  0.0 381.7 jit_solution(4261685247920140671)
XLA Ops:
  7.2 4.4 %fusion.51 = (bf16[1,1,2048,512]{3,2,1,0:T(8,128)(2,1)}, bf16[1,1,2048,512]{3,2,1,0:T(8,128)(2,1)}) fusion(bf16[2,1,2048,512]{3,2,1,0:T(8,128)(2,1)} %param.20), kind=kLoop, calls=%fused_computation.70 | loop fusion | bytes 8388608 | tf_op jit(solution)/shard_map/slice | solution.py:88
  11.6 2.9 copy.79
  16.5 3.3 reshape_reshape.3
  19.8 4.0 %copy.80 = bf16[1,1,2048,512]{2,3,1,0:T(8,128)(2,1)} copy(bf16[1,1,2048,512]{3,2,1,0:T(8,128)(2,1)} %get-tuple-element.6) | data formatting | bytes 4194304
  24.2 10.5 %fusion = (f32[2,2,576]{2,1,0:T(2,128)}, f32[2,2048,576,2]{1,2,3,0:T(8,128)}) fusion(f32[576,2048]{1,0:T(8,128)S(1)} %broadcast_multiply_fusion, bf16[2048,2,256,1]{0,2,3,1:T(8,128)(2,1)S(1)} %bitcast.83, bf16[576,2,2,256]{3,2,1,0:T(2,128)(2,1)S(1)} %reshape_reshape.3), kind=kOutput, calls=%fused_computation.1 | convolution fusion | flops 2434791168 | bytes 26878976 | tf_op jit(solution)/shard_map/qhrd,khd->hrqk/dot_general | solution.py:33
  34.7 9.1 %fusion.6 = f32[576,2,2,256]{3,0,2,1:T(8,128)S(1)} fusion(bf16[2048,2,256,1]{0,2,3,1:T(8,128)(2,1)S(1)} %bitcast.85, f32[2,2048,576,2]{1,2,3,0:T(8,128)} %get-tuple-element.15, f32[576,2048]{1,0:T(8,128)S(1)} %broadcast_multiply_fusion), kind=kOutput, calls=%fused_computation.10 | convolution fusion | flops 2434793472 | bytes 28049408 | tf_op jit(solution)/shard_map/hrqk,khd->qhrd/dot_general | solution.py:38
  43.8 1.8 copy.56
  45.6 2.9 reshape.101
  48.6 0.7 all-gather.3.cloned.1.call-update
  49.8 0.9 reshape.102
  50.7 0.7 reshape.104
  51.7 1.4 convolution_minimum_fusion.5
  53.5 0.4 convolution_minimum_fusion.3
  53.9 0.4 convolution_minimum_fusion.2
  54.4 0.4 convolution_minimum_fusion.1
  54.8 0.4 convolution_minimum_fusion
  55.3 0.9 fusion.53
  56.3 124.9 %psum.38 = f32[576,4]{0,1:T(4,128)S(1)} all-reduce(f32[576,4]{0,1:T(4,128)S(1)} %reshape.104), channel_id=1, replica_groups=mesh['blk'=32,'mp'=4] {'blk'}, use_global_device_ids=true, to_apply=%region_6.7 | all-reduce | flops 2304 | bytes 18432 | tf_op jit(solution)/shard_map/psum | solution.py:99
  181.7 0.5 convolution_bitcast_fusion
  182.2 1.8 copy.62
  184.1 2.9 reshape.103
  187.1 5.1 %fusion.39 = f32[18,3584]{1,0:T(8,128)} fusion(bf16[1024,3584]{1,0:T(8,128)(2,1)} %param.25, f32[18,1024]{1,0:T(8,128)S(1)} %bitcast.87, f32[576,1024]{1,0:T(8,128)} %reshape.103, s32[]{:T(128)S(6)} %select_n.25, f32[576,1024]{1,0:T(8,128)} %all-reduce.4.cloned.1.call-done), kind=kOutput, calls=%fused_computation.47 | convolution fusion | flops 132175872 | bytes 7868420 | tf_op jit(solution)/shard_map/dot_general | solution.py:118
  192.4 32.7 %all-gather.3.cloned.1.call-done = bf16[2,3584,896]{2,1,0:T(8,128)(2,1)} async-done(((bf16[2,112,896]{2,1,0:T(8,128)(2,1)}), bf16[2,3584,896]{2,1,0:T(8,128)(2,1)}) %all-gather.3.cloned.1.call-update) | async-done | bytes 12845072 | tf_op jit(solution)/shard_map/all_gather | solution.py:67
  225.2 7.6 %add_convert_fusion = bf16[2,144,896]{2,1,0:T(8,128)(2,1)} fusion(bf16[2,3584,896]{2,1,0:T(8,128)(2,1)} %all-gather.3.cloned.1.call-done, bf16[144,3584]{1,0:T(8,128)(2,1)S(1)} %copy-done.4, f32[144,896]{1,0:T(8,128)S(1)} %dynamic-slice_convert_fusion), kind=kOutput, calls=%fused_computation.32 | convolution fusion | flops 1851236352 | bytes 14909440 | tf_op jit(solution)/shard_map/rd,mdu->mru/dot_general | solution.py:64
  232.8 34.1 %all-reduce.6.cloned.1.call-done = f32[18,3584]{1,0:T(8,128)} async-done(((f32[18,3584]{1,0:T(8,128)}), f32[18,3584]{1,0:T(8,128)}) %all-reduce.6.cloned.1.call-update) | async-done | bytes 258064 | tf_op jit(solution)/shard_map/psum | solution.py:118
  266.9 1.1 multiply_reduce_fusion
  268.0 1.8 add_convert_fusion.1
  269.8 31.7 %all-gather.5.cloned.1.call-done = bf16[2,144,3584]{2,1,0:T(8,128)(2,1)} async-done(((bf16[2,144,896]{2,1,0:T(8,128)(2,1)}), bf16[2,144,3584]{2,1,0:T(8,128)(2,1)}) %all-gather.5.cloned.1.call-update) | async-done | bytes 2064400 | tf_op jit(solution)/shard_map/all_gather | solution.py:74
  301.5 6.2 %exponential_reduce_fusion = (f32[2,144]{1,0:T(2,128)S(1)}, f32[2,144,1024]{2,1,0:T(8,128)S(1)}) fusion(bf16[2,144,3584]{2,1,0:T(8,128)(2,1)} %all-gather.5.cloned.1.call-done, bf16[1024,3584]{1,0:T(8,128)(2,1)} %param.16), kind=kOutput, calls=%fused_computation.24 | convolution fusion | flops 2114813696 | bytes 10585216 | tf_op jit(solution)/shard_map/mrd,vd->mrv/dot_general | solution.py:76
  307.8 1.8 select_reduce_fusion
  309.6 64.9 %all-reduce = (f32[2,144,10]{1,2,0:T(8,128)S(1)}, f32[2,144]{1,0:T(2,128)S(1)}) all-reduce(f32[2,144,10]{1,2,0:T(8,128)S(1)} %select_reduce_fusion, f32[2,144]{1,0:T(2,128)S(1)} %get-tuple-element.10), channel_id=1, replica_groups=mesh['blk'=32,'mp'=4] {'blk','mp'}, use_global_device_ids=true, to_apply=%region_1.2 | all-reduce | flops 3168 | bytes 25344 | tf_op jit(solution)/shard_map/psum | solution.py:84
  374.5 0.6 copy.65
  (45 shorter events, 2.7 us)
Async XLA Ops:
  7.2 179.9 %all-reduce.4.cloned.1.call-start = ((), (), s32[]{:S(2)}) async-start(), calls=%async_computation.2 | async-start | bytes 4718592 | tf_op jit(solution)/shard_map/psum | solution.py:99
  24.2 10.5 %copy-start.1 = (bf16[1,1,2048,512]{2,3,1,0:T(8,128)(2,1)S(1)}, bf16[1,1,2048,512]{2,3,1,0:T(8,128)(2,1)}, u32[]{:S(2)}) copy-start(bf16[1,1,2048,512]{2,3,1,0:T(8,128)(2,1)} %copy.80) | copy-start | bytes 6291460
  48.6 1.3 copy-start
  48.6 2.9 copy-start.2
  48.6 176.6 %all-gather.3.cloned.1.call-start = ((), (), s32[]{:S(2)}) async-start(), calls=%async_computation | async-start | bytes 13246464 | tf_op jit(solution)/shard_map/all_gather | solution.py:67
  49.3 217.6 %all-reduce.6.cloned.1.call-start = ((), (), s32[]{:S(2)}) async-start(), calls=%async_computation.3 | async-start | bytes 688128 | tf_op jit(solution)/shard_map/psum | solution.py:118
  184.0 3.0 copy-start.4
  192.1 40.7 %copy-start.5 = (s32[2,144,10]{1,0,2:T(2,128)S(1)}, s32[2,144,10]{1,0,2:T(2,128)}, u32[]{:S(2)}) copy-start(s32[2,144,10]{1,0,2:T(2,128)} %param.17) | copy-start | bytes 34564
  192.2 75.9 %copy-start.3 = (bf16[18,3584]{1,0:T(8,128)(2,1)S(1)}, bf16[18,3584]{1,0:T(8,128)(2,1)}, u32[]{:S(2)}) copy-start(bf16[18,3584]{1,0:T(8,128)(2,1)} %param.27) | copy-start | bytes 387076
  192.2 75.9 %copy-start.6 = (f32[3584]{0:T(1024)S(1)}, f32[3584]{0:T(1024)}, u32[]{:S(2)}) copy-start(f32[3584]{0:T(1024)} %param.26) | copy-start | bytes 43012
  192.2 109.4 %all-gather.5.cloned.1.call-start = ((), (), s32[]{:S(2)}) async-start(), calls=%async_computation.1 | async-start | bytes 2580480 | tf_op jit(solution)/shard_map/all_gather | solution.py:74
Sparse Core Ops, SparseCore 0:
  48.7 110.4 all-reduce.3
  161.6 63.5 all-gather.2
  227.5 39.3 all-reduce.5
  268.4 33.0 all-gather.4
where the time goes:
time: 382 us
  blocking collectives  190 us (50%)
  waiting for transfers between devices  99.3 us (26%)
  matrix products  43.3 us (11%)
  local copies, waits for them, and re-layouts  27.5 us (7%)
  between operations  16 us (4%)
  other arithmetic  5.25 us (1%)
    psum x1, blocking collectives, per_device(): summed = lax.psum((numer, denom), 'blk')  125 us
    psum x1, blocking collectives, per_device(): totals, picked = lax.psum((totals, picked), ('blk', 'mp'))  64.9 us
    psum x1, waiting for transfers between devices, per_device(): lax.psum(jnp.dot(heads_out, out_weight, preferred_element_type=jnp.float3...  34.1 us
    all_gather x1, waiting for transfers between devices, per_device(): lax.all_gather(medusa_w, 'blk', axis=1, tiled=True)  32.7 us
    all_gather x1, waiting for transfers between devices, per_device(): full_fresh = lax.all_gather(fresh, 'mp', axis=2, tiled=True)  31.7 us
    dot_general x2, matrix products, attend(): jnp.einsum('qhrd,khd->hrqk', query_view, key_view, preferred_element_type...  11.3 us
    dot_general x2, matrix products, attend(): jnp.einsum('hrqk,khd->qhrd', weights.astype(jnp.bfloat16), value_view, pr...  9.63 us
    unnamed x19, local copies, waits for them, and re-layouts  7.84 us
  transfers between devices with their start and end apart: 4, of which 3 were waited for; matrix products, arithmetic and copies ran while one was open for 7% of the time, Pallas kernels for 0%

commit v1 on v0

--- a/solution.py
+++ b/solution.py
@@ -4,6 +4,12 @@
 from jax.sharding import PartitionSpec as P
 
 HEAD_SIZE = 256
+_obtain_trees = lambda vals: jnp.concatenate(
+    jax.lax.all_to_all(
+        jnp.stack([vals for _ in range(jax.lax.psum(1, "blk"))], axis=0), "blk", 0, 0
+    ),
+    axis=1,
+)
 
 
 def capped(values, limit):
@@ -62,10 +68,7 @@
 ):
     units = medusa_w.shape[2]
     inner = jnp.einsum(
-        "rd,mdu->mru",
-        hidden,
-        lax.all_gather(medusa_w, "blk", axis=1, tiled=True),
-        preferred_element_type=jnp.float32,
+        "rd,mdu->mru", hidden, _obtain_trees(medusa_w), preferred_element_type=jnp.float32
     )
     own_cols = lax.dynamic_slice_in_dim(hidden, lax.axis_index("mp") * units, units, 1).astype(
         jnp.float32

time: 382 us -> 459 us (1.20)
  blocking collectives: 190 us -> 283 us
  waiting for transfers between devices: 99.3 us -> 64.8 us
  local copies, waits for them, and re-layouts: 27.5 us -> 42 us
  starting transfers between devices: 0.56 us -> 9.17 us
  matrix products: 43.3 us -> 38.7 us
    psum x1, blocking collectives: 125 us -> 218 us  [per_device(): summed = lax.psum((numer, denom), 'blk')]
    all_gather x1 -> x0, waiting for transfers between devices: 32.7 us -> none  [per_device(): lax.all_gather(medusa_w, 'blk', axis=1, tiled=True)]
    all_to_all x0 -> x1, starting transfers between devices: none -> 8.64 us  [jax.lax.all_to_all(jnp.stack([vals for _ in range(jax.lax.psum(1, 'blk'))...]
    another operation x0 -> x1, local copies, waits for them, and re-layouts: none -> 6.58 us  [jnp.stack([vals for _ in range(jax.lax.psum(1, 'blk'))], axis=0)]
    reshape x0 -> x1, local copies, waits for them, and re-layouts: none -> 6.38 us  [jnp.concatenate(jax.lax.all_to_all(jnp.stack([vals for _ in range(jax.lax...]
  transfers between devices with their start and end apart: 4 -> 4, of which waited for: 3 -> 2; matrix products, arithmetic and copies ran while one was open for 7% -> 15% of each run, Pallas kernels for 0% -> 0%
where the time goes in v1:
time: 459 us
  blocking collectives  283 us (62%)
  waiting for transfers between devices  64.8 us (14%)
  local copies, waits for them, and re-layouts  42 us (9%)
  matrix products  38.7 us (8%)
  between operations  16 us (3%)
  starting transfers between devices  9.17 us (2%)
  other arithmetic  5.25 us (1%)
    psum x1, blocking collectives, per_device(): summed = lax.psum((numer, denom), 'blk')  218 us
    psum x1, blocking collectives, per_device(): totals, picked = lax.psum((totals, picked), ('blk', 'mp'))  64.9 us
    psum x1, waiting for transfers between devices, per_device(): lax.psum(jnp.dot(heads_out, out_weight, preferred_element_type=jnp.float3...  32.9 us
    all_gather x1, waiting for transfers between devices, per_device(): full_fresh = lax.all_gather(fresh, 'mp', axis=2, tiled=True)  31.9 us
    dot_general x2, matrix products, attend(): jnp.einsum('qhrd,khd->hrqk', query_view, key_view, preferred_element_type...  12 us
    dot_general x2, matrix products, attend(): jnp.einsum('hrqk,khd->qhrd', weights.astype(jnp.bfloat16), value_view, pr...  9.63 us
  transfers between devices with their start and end apart: 4, of which 2 were waited for; matrix products, arithmetic and copies ran while one was open for 15% of the time, Pallas kernels for 0%

profile of v1, /device:TPU:1, one launch (start us, length us, event | category | flops | bytes accessed | tf_op | source)
XLA Modules:
  0.0 458.6 jit_solution(8715307443991996291)
XLA Ops:
  7.2 6.6 %stack.2 = bf16[32,2,112,896]{3,2,1,0:T(8,128)(2,1)} broadcast(bf16[2,112,896]{2,1,0:T(8,128)(2,1)} %param.15), dimensions={1,2,3} | broadcast | bytes 13246464 | tf_op jit(solution)/shard_map/stack | solution.py:9
  13.7 8.6 %all-to-all-start = ((bf16[32,2,112,896]{3,2,1,0:T(8,128)(2,1)}), bf16[32,2,112,896]{3,2,1,0:T(8,128)(2,1)}, u32[]{:S(2)}, u32[]{:S(2)}) async-start(bf16[32,2,112,896]{3,2,1,0:T(8,128)(2,1)} %stack.2), calls=%async_computation | async-start | bytes 25690112 | tf_op jit(solution)/shard_map/all_to_all | solution.py:8
  22.4 4.4 fusion.51
  26.9 2.9 copy.81
  31.7 3.3 reshape_reshape.3
  35.1 4.0 copy.82
  39.4 9.9 %fusion = (f32[2,2,576]{2,1,0:T(2,128)S(1)}, f32[2,2048,576,2]{1,2,3,0:T(8,128)}) fusion(f32[576,2048]{1,0:T(8,128)S(1)} %broadcast_multiply_fusion, bf16[2048,2,256,1]{0,2,3,1:T(8,128)(2,1)S(1)} %bitcast.86, bf16[576,2,2,256]{3,2,1,0:T(2,128)(2,1)S(1)} %reshape_reshape.3), kind=kOutput, calls=%fused_computation.1 | convolution fusion | flops 2434791168 | bytes 26878976 | tf_op jit(solution)/shard_map/qhrd,khd->hrqk/dot_general | solution.py:39
  49.3 9.1 %fusion.6 = f32[576,2,2,256]{3,0,2,1:T(8,128)S(1)} fusion(bf16[2048,2,256,1]{0,2,3,1:T(8,128)(2,1)S(1)} %bitcast.88, f32[2,2048,576,2]{1,2,3,0:T(8,128)} %get-tuple-element.15, f32[576,2048]{1,0:T(8,128)S(1)} %broadcast_multiply_fusion), kind=kOutput, calls=%fused_computation.10 | convolution fusion | flops 2434793472 | bytes 28049408 | tf_op jit(solution)/shard_map/hrqk,khd->qhrd/dot_general | solution.py:44
  58.4 1.8 copy.58
  60.3 2.9 reshape.111
  63.9 0.6 convolution_minimum_fusion.5
  64.5 0.4 convolution_minimum_fusion.4
  64.9 0.4 convolution_minimum_fusion.3
  65.3 0.4 convolution_minimum_fusion.2
  65.8 1.3 fusion.52
  67.5 1.7 reshape.112
  70.0 2.2 fusion.53
  72.2 217.7 %psum.38 = f32[576,4]{0,1:T(4,128)S(1)} all-reduce(f32[576,4]{0,1:T(4,128)S(1)} %reshape.114), channel_id=1, replica_groups=mesh['blk'=32,'mp'=4] {'blk'}, use_global_device_ids=true, to_apply=%region_6.7 | all-reduce | flops 2304 | bytes 18432 | tf_op jit(solution)/shard_map/psum | solution.py:102
  290.4 0.5 convolution_bitcast_fusion
  290.9 1.8 copy.64
  292.7 2.9 reshape.113
  295.8 5.1 %fusion.39 = f32[18,3584]{1,0:T(8,128)} fusion(bf16[1024,3584]{1,0:T(8,128)(2,1)} %param.25, f32[18,1024]{1,0:T(8,128)S(1)} %bitcast.90, f32[576,1024]{1,0:T(8,128)} %reshape.113, s32[]{:T(128)S(6)} %select_n.25, f32[576,1024]{1,0:T(8,128)} %all-reduce.4.cloned.1.call-done), kind=kOutput, calls=%fused_computation.47 | convolution fusion | flops 132175872 | bytes 7868420 | tf_op jit(solution)/shard_map/dot_general | solution.py:121
  301.1 6.4 %copy.52 = bf16[2,32,112,896]{3,2,1,0:T(8,128)(2,1)S(1)} copy(bf16[2,32,112,896]{3,2,0,1:T(8,128)(2,1)} %bitcast) | data formatting | bytes 25690112 | tf_op jit(solution)/shard_map/reshape | solution.py:7
  307.5 3.1 add_convert_fusion
  310.7 32.9 %all-reduce.6.cloned.1.call-done = f32[18,3584]{1,0:T(8,128)} async-done(((f32[18,3584]{1,0:T(8,128)}), f32[18,3584]{1,0:T(8,128)}) %all-reduce.6.cloned.1.call-update) | async-done | bytes 258064 | tf_op jit(solution)/shard_map/psum | solution.py:121
  343.6 1.1 multiply_reduce_fusion
  344.8 1.8 add_convert_fusion.1
  346.5 31.9 %all-gather.2.cloned.1.call-done = bf16[2,144,3584]{2,1,0:T(8,128)(2,1)} async-done(((bf16[2,144,896]{2,1,0:T(8,128)(2,1)}), bf16[2,144,3584]{2,1,0:T(8,128)(2,1)}) %all-gather.2.cloned.1.call-update) | async-done | bytes 2064400 | tf_op jit(solution)/shard_map/all_gather | solution.py:77
  378.4 6.2 %exponential_reduce_fusion = (f32[2,144]{1,0:T(2,128)S(1)}, f32[2,144,1024]{2,1,0:T(8,128)S(1)}) fusion(bf16[2,144,3584]{2,1,0:T(8,128)(2,1)} %all-gather.2.cloned.1.call-done, bf16[1024,3584]{1,0:T(8,128)(2,1)} %param.16), kind=kOutput, calls=%fused_computation.24 | convolution fusion | flops 2114813696 | bytes 10585216 | tf_op jit(solution)/shard_map/mrd,vd->mrv/dot_general | solution.py:79
  384.6 1.8 select_reduce_fusion
  386.5 64.9 %all-reduce = (f32[2,144,10]{1,2,0:T(8,128)S(1)}, f32[2,144]{1,0:T(2,128)S(1)}) all-reduce(f32[2,144,10]{1,2,0:T(8,128)S(1)} %select_reduce_fusion, f32[2,144]{1,0:T(2,128)S(1)} %get-tuple-element.10), channel_id=1, replica_groups=mesh['blk'=32,'mp'=4] {'blk','mp'}, use_global_device_ids=true, to_apply=%region_1.2 | all-reduce | flops 3168 | bytes 25344 | tf_op jit(solution)/shard_map/psum | solution.py:87
  451.4 0.6 copy.67
  (46 shorter events, 3.1 us)
Async XLA Ops:
  13.7 287.4 %all-to-all-start = ((bf16[32,2,112,896]{3,2,1,0:T(8,128)(2,1)}), bf16[32,2,112,896]{3,2,1,0:T(8,128)(2,1)}, u32[]{:S(2)}, u32[]{:S(2)}) async-start(bf16[32,2,112,896]{3,2,1,0:T(8,128)(2,1)} %stack.2), calls=%async_computation | async-start | bytes 25690112 | tf_op jit(solution)/shard_map/all_to_all | solution.py:8
  22.4 273.4 %all-reduce.4.cloned.1.call-start = ((), (), s32[]{:S(2)}) async-start(), calls=%async_computation.2 | async-start | bytes 4718592 | tf_op jit(solution)/shard_map/psum | solution.py:102
  39.4 9.9 %copy-start.1 = (bf16[1,1,2048,512]{2,3,1,0:T(8,128)(2,1)S(1)}, bf16[1,1,2048,512]{2,3,1,0:T(8,128)(2,1)}, u32[]{:S(2)}) copy-start(bf16[1,1,2048,512]{2,3,1,0:T(8,128)(2,1)} %copy.82) | copy-start | bytes 6291460
  63.2 0.7 copy-start.6
  63.2 280.4 %all-reduce.6.cloned.1.call-start = ((), (), s32[]{:S(2)}) async-start(), calls=%async_computation.3 | async-start | bytes 688128 | tf_op jit(solution)/shard_map/psum | solution.py:121
  64.9 2.6 copy-start
  292.7 3.0 copy-start.3
  300.8 77.5 %all-gather.2.cloned.1.call-start = ((), (), s32[]{:S(2)}) async-start(), calls=%async_computation.1 | async-start | bytes 2580480 | tf_op jit(solution)/shard_map/all_gather | solution.py:77
  307.5 3.2 copy-start.4
  307.5 37.2 %copy-start.2 = (bf16[18,3584]{1,0:T(8,128)(2,1)S(1)}, bf16[18,3584]{1,0:T(8,128)(2,1)}, u32[]{:S(2)}) copy-start(bf16[18,3584]{1,0:T(8,128)(2,1)} %param.27) | copy-start | bytes 387076
  307.5 37.2 %copy-start.5 = (f32[3584]{0:T(1024)S(1)}, f32[3584]{0:T(1024)}, u32[]{:S(2)}) copy-start(f32[3584]{0:T(1024)} %param.26) | copy-start | bytes 43012
Sparse Core Ops, SparseCore 0:
  63.3 209.1 all-reduce.3
  301.0 42.5 all-reduce.5
  345.3 33.0 all-gather.1
